TPU v7x, 128 devices: a whole 4x4x4 slice. The times are simulated.
128 devices in a mesh: shot: 4 (over y_lo, core), gx: 4 (over z), gy: 8 (over x, y_hi).
Axes of the slice: x: 4, y: 4 (y_hi: 2, y_lo: 2; y = y_hi * 2 + y_lo), z: 4, core: 2. Of those that a mesh axis runs over, the one named last changes fastest.
Arguments:
- model_tiles: float32 [256, 256, 128], P(('shot', 'gx'), 'gy'), may hold values from 0.2 to 0.45
- owner_map: int32 [16], replicated, may hold values from 0 to 15, each once
- offsets: int32 [4], P('shot'), may hold values from 0 to 12
- field_now: float32 [4, 2, 64, 256, 128], P('shot', None, 'gx', 'gy'), may hold values from -6 to 6
- field_prev: float32 [4, 2, 64, 256, 128], P('shot', None, 'gx', 'gy'), may hold values from -6 to 6
- sources: int32 [4, 2, 3], P('shot'), may hold values from 0 to 255, as said below
- wavelet: float32 [4, 2, 8], P('shot'), may hold values from -6 to 6
- receivers: int32 [4, 256, 3], P('shot'), may hold values from 0 to 255, as said below
Outputs:
- out_now: float32 [4, 2, 64, 256, 128], P('shot', None, 'gx', 'gy')
- out_prev: float32 [4, 2, 64, 256, 128], P('shot', None, 'gx', 'gy')
- traces: float32 [4, 2, 256, 8], P('shot')
Inputs may be any that keep to these rules, and one draw needn't show every extreme that they name: `sources`: each row is a cell of the group's aperture: first entry below 64, second below 256, third below 128. `receivers`: each row is a cell of the group's aperture: first entry below 64, second below 256, third below 128.
All inputs are finite; a program needn't handle non-finite values.
Results may differ from a plain program's by a relative error of at most 0.0003.
Values sent between devices are 32-bit elements; how exact they have to be, the bound alone decides.
A program may use at most 128 MiB of HBM per device.

v0:
```python
import jax
import jax.numpy as jnp
from jax import lax
from jax.sharding import PartitionSpec as P

STEPS = 8
center_weight = -2.5
near_weight = 4.0 / 3.0
far_weight = -1.0 / 12.0
damp_peak = 0.3


def extended_2(cells, sides, width):
    for axis, dim in sides:
        count = lax.axis_size(axis)
        ends = count - 1
        head = lax.slice_in_dim(cells, 0, width, axis=dim)
        tail = lax.slice_in_dim(cells, cells.shape[dim] - width, cells.shape[dim], axis=dim)
        cells = jnp.concatenate(
            [
                lax.ppermute(tail, axis, [(i, (i + 1) % count) for i in range(ends)]),
                cells,
                lax.ppermute(head, axis, [((i + 1) % count, i) for i in range(ends)]),
            ],
            axis=dim,
        )
    return cells


def depth_ahead(field, reach):
    filler = jnp.zeros(field.shape[:-1] + (reach,), field.dtype)
    return jnp.concatenate([field[..., reach:], filler], axis=-1)


def depth_behind(field, reach):
    filler = jnp.zeros(field.shape[:-1] + (reach,), field.dtype)
    return jnp.concatenate([filler, field[..., :-reach]], axis=-1)


def laplace(extended):
    middle = extended[:, 2:-2, 2:-2]
    along_x = (
        center_weight * middle
        + near_weight * (extended[:, 3:-1, 2:-2] + extended[:, 1:-3, 2:-2])
        + far_weight * (extended[:, 4:, 2:-2] + extended[:, :-4, 2:-2])
    )
    along_y = (
        center_weight * middle
        + near_weight * (extended[:, 2:-2, 3:-1] + extended[:, 2:-2, 1:-3])
        + far_weight * (extended[:, 2:-2, 4:] + extended[:, 2:-2, :-4])
    )
    along_z = (
        center_weight * middle
        + near_weight * (depth_ahead(middle, 1) + depth_behind(middle, 1))
        + far_weight * (depth_ahead(middle, 2) + depth_behind(middle, 2))
    )
    return along_x + along_y + along_z


def damping(x_cells, y_cells, width, x_total, y_total):
    x_depth = (
        jnp.maximum(width - jnp.minimum(x_cells + 1, x_total - x_cells), 0).astype(jnp.float32)
        / width
    )
    y_depth = (
        jnp.maximum(width - jnp.minimum(y_cells + 1, y_total - y_cells), 0).astype(jnp.float32)
        / width
    )
    return damp_peak * (x_depth[:, None] * x_depth[:, None] + y_depth[None, :] * y_depth[None, :])


def injection(x_cells, y_cells, z_cells, source_cells, amplitude):
    on_x = (x_cells[None, :] == source_cells[:, 0:1]).astype(jnp.float32)
    on_y = (y_cells[None, :] == source_cells[:, 1:2]).astype(jnp.float32)
    on_z = (z_cells[None, :] == source_cells[:, 2:3]).astype(jnp.float32)
    return (
        amplitude[:, None, None, None]
        * on_x[:, :, None, None]
        * on_y[:, None, :, None]
        * on_z[:, None, None, :]
    )


def advance(extended, previous, coef, damp, inject):
    middle = extended[:, 2:-2, 2:-2]
    return (2.0 * middle - (1.0 - damp) * previous + coef * laplace(extended) + inject) / (
        1.0 + damp
    )


def sample(field, receiver_cells, x_start, y_start):
    size_x, size_y = (field.shape[1], field.shape[2])
    local_x = receiver_cells[:, 0] - x_start
    local_y = receiver_cells[:, 1] - y_start
    inside = (local_x >= 0) & (local_x < size_x) & (local_y >= 0) & (local_y < size_y)
    values = field[
        :, jnp.clip(local_x, 0, size_x - 1), jnp.clip(local_y, 0, size_y - 1), receiver_cells[:, 2]
    ]
    return jnp.where(inside[None, :], values, 0.0)


def local(model_tiles, owner_map, offsets, field_now, field_prev, sources, wavelet, receivers):
    block_x, block_y, depth = model_tiles.shape
    column_index = lax.axis_index("gx")
    row_index = lax.axis_index("gy")
    across = lax.axis_size("gx")
    total_x = block_x * across
    total_y = block_y * lax.axis_size("gy")
    shift_x = offsets[0]
    tile_total = owner_map.shape[0]
    column_ids = jnp.arange(tile_total, dtype=jnp.int32)
    wanted = jnp.sum(jnp.where(column_ids == shift_x + column_index, owner_map, 0))
    piece = lax.all_gather(model_tiles, ("shot", "gx"), axis=0, tiled=True)
    rows = wanted * block_x + jnp.arange(block_x, dtype=jnp.int32)
    inside = (rows >= 0) & (rows < piece.shape[0])
    taken = jnp.take(piece, jnp.clip(rows, 0, piece.shape[0] - 1), axis=0)
    speed = jnp.where(inside[:, None, None], taken, jnp.zeros_like(model_tiles))
    coef = speed * speed
    current = field_now[0]
    previous = field_prev[0]
    source_cells = sources[0]
    amplitudes = wavelet[0]
    receiver_cells = receivers[0]
    x_start = column_index * block_x
    y_start = row_index * block_y
    x_here = x_start + jnp.arange(block_x, dtype=jnp.int32)
    y_here = y_start + jnp.arange(block_y, dtype=jnp.int32)
    z_cells = jnp.arange(depth, dtype=jnp.int32)
    damp = damping(x_here, y_here, block_x, total_x, total_y)[:, :, None]
    recorded = []
    for step in range(STEPS):
        extended = extended_2(current, (("gx", 1), ("gy", 2)), 2)
        inject = injection(x_here, y_here, z_cells, source_cells, amplitudes[:, step])
        fresh = advance(extended, previous, coef, damp, inject)
        recorded.append(sample(fresh, receiver_cells, x_start, y_start))
        previous = current
        current = fresh
    traces = lax.psum(jnp.stack(recorded, axis=-1), ("gx", "gy"))
    return (current[None], previous[None], traces[None])


def solution(mesh):
    return jax.shard_map(
        local,
        mesh=mesh,
        in_specs=(
            P(("shot", "gx"), "gy", None),
            P(),
            P("shot"),
            P("shot", None, "gx", "gy", None),
            P("shot", None, "gx", "gy", None),
            P("shot", None, None),
            P("shot", None, None),
            P("shot", None, None),
        ),
        out_specs=(
            P("shot", None, "gx", "gy", None),
            P("shot", None, "gx", "gy", None),
            P("shot", None, None, None),
        ),
        check_vma=False,
    )
```

profile of v0, /device:TPU:0, one launch (start us, length us, event | category | flops | bytes accessed | tf_op | source)
XLA Modules:
  0.0 552.9 jit_solution(16876477504030605119)
XLA Ops:
  8.8 1.3 collective-permute-start
  10.1 4.5 collective-permute-start.1
  15.3 1.3 fusion.155
  21.3 2.2 fusion.179
  23.5 2.3 fusion.178
  26.9 1.3 collective-permute-start.2
  28.2 6.1 %collective-permute-start.3 = (f32[2,20,2,128]{3,2,1,0:T(2,128)S(1)}, f32[2,20,2,128]{3,2,1,0:T(2,128)S(1)}, u32[]{:S(2)}, u32[]{:S(2)}) collective-permute-start(f32[2,20,2,128]{3,2,1,0:T(2,128)S(1)} %get-tuple-element.57), channel_id=1, source_target_pairs={{0,1},{1,2},{2,3},{3,4},{4,5},{5,6},{6,7},{8,9},{9,10},{10,11},{11... | collective-permute-start | bytes 122888 | tf_op jit(solution)/shard_map/ppermute | solution.py:21
  34.7 1.5 collective-permute-done.3
  36.1 1.4 pad_maximum_fusion
  37.5 24.6 %all-gather.2.cloned.1.call-done = f32[256,32,128]{2,1,0:T(8,128)} async-done(((f32[16,32,128]{2,1,0:T(8,128)}), f32[256,32,128]{2,1,0:T(8,128)}) %all-gather.2.cloned.1.call-update) | async-done | bytes 4194320 | tf_op jit(solution)/shard_map/all_gather | solution.py:113
  62.1 2.7 gather_fusion
  65.0 3.1 fusion.94
  68.1 1.3 collective-permute-start.4
  69.4 4.5 collective-permute-start.5
  76.1 1.3 collective-permute-start.6
  77.4 6.1 %collective-permute-start.7 = (f32[2,20,2,128]{3,2,1,0:T(2,128)S(1)}, f32[2,20,2,128]{3,2,1,0:T(2,128)S(1)}, u32[]{:S(2)}, u32[]{:S(2)}) collective-permute-start(f32[2,20,2,128]{3,2,1,0:T(2,128)S(1)} %get-tuple-element.53), channel_id=1, source_target_pairs={{0,1},{1,2},{2,3},{3,4},{4,5},{5,6},{6,7},{8,9},{9,10},{10,11},{11... | collective-permute-start | bytes 122888 | tf_op jit(solution)/shard_map/ppermute | solution.py:21
  84.4 16.7 %copy.515 = f32[2,16,32,128]{0,3,2,1:T(8,128)} copy(f32[2,16,32,128]{3,2,1,0:T(8,128)S(1)} %fusion.94) | data formatting | bytes 1048576 | tf_op jit(solution)/shard_map/div | solution.py:86
  101.0 3.0 gather_fusion.1
  104.2 2.0 fusion.82
  106.2 1.3 collective-permute-start.8
  107.5 5.0 collective-permute-start.9
  112.8 1.6 collective-permute-done.9
  114.5 1.3 collective-permute-start.10
  115.8 6.5 %collective-permute-start.11 = (f32[2,20,2,128]{3,2,1,0:T(2,128)S(1)}, f32[2,20,2,128]{3,2,1,0:T(2,128)S(1)}, u32[]{:S(2)}, u32[]{:S(2)}) collective-permute-start(f32[2,20,2,128]{3,2,1,0:T(2,128)S(1)} %get-tuple-element.49), channel_id=1, source_target_pairs={{0,1},{1,2},{2,3},{3,4},{4,5},{5,6},{6,7},{8,9},{9,10},{10,11},{11... | collective-permute-start | bytes 122888 | tf_op jit(solution)/shard_map/ppermute | solution.py:21
  123.2 16.7 %copy.516 = f32[2,16,32,128]{0,3,2,1:T(8,128)} copy(f32[2,16,32,128]{3,2,1,0:T(8,128)S(1)} %fusion.82) | data formatting | bytes 1048576 | tf_op jit(solution)/shard_map/div | solution.py:86
  139.9 3.0 gather_fusion.2
  143.1 2.0 fusion.70
  145.1 1.3 collective-permute-start.12
  146.4 4.9 collective-permute-start.13
  151.6 1.6 collective-permute-done.13
  153.2 1.3 collective-permute-start.14
  154.5 6.9 %collective-permute-start.15 = (f32[2,20,2,128]{3,2,1,0:T(2,128)S(1)}, f32[2,20,2,128]{3,2,1,0:T(2,128)S(1)}, u32[]{:S(2)}, u32[]{:S(2)}) collective-permute-start(f32[2,20,2,128]{3,2,1,0:T(2,128)S(1)} %get-tuple-element.45), channel_id=1, source_target_pairs={{0,1},{1,2},{2,3},{3,4},{4,5},{5,6},{6,7},{8,9},{9,10},{10,11},{11... | collective-permute-start | bytes 122888 | tf_op jit(solution)/shard_map/ppermute | solution.py:21
  162.4 16.7 %copy.517 = f32[2,16,32,128]{0,3,2,1:T(8,128)} copy(f32[2,16,32,128]{3,2,1,0:T(8,128)S(1)} %fusion.70) | data formatting | bytes 1048576 | tf_op jit(solution)/shard_map/div | solution.py:86
  179.1 3.0 gather_fusion.3
  182.3 2.0 fusion.58
  184.3 1.3 collective-permute-start.16
  185.6 4.9 collective-permute-start.17
  190.7 1.6 collective-permute-done.17
  193.7 7.1 %collective-permute-start.19 = (f32[2,20,2,128]{3,2,1,0:T(2,128)S(1)}, f32[2,20,2,128]{3,2,1,0:T(2,128)S(1)}, u32[]{:S(2)}, u32[]{:S(2)}) collective-permute-start(f32[2,20,2,128]{3,2,1,0:T(2,128)S(1)} %get-tuple-element.41), channel_id=1, source_target_pairs={{0,1},{1,2},{2,3},{3,4},{4,5},{5,6},{6,7},{8,9},{9,10},{10,11},{11... | collective-permute-start | bytes 122888 | tf_op jit(solution)/shard_map/ppermute | solution.py:21
  201.7 16.7 %copy.518 = f32[2,16,32,128]{0,3,2,1:T(8,128)} copy(f32[2,16,32,128]{3,2,1,0:T(8,128)S(1)} %fusion.58) | data formatting | bytes 1048576 | tf_op jit(solution)/shard_map/div | solution.py:86
  218.4 3.0 gather_fusion.4
  221.6 2.0 fusion.46
  224.9 4.9 collective-permute-start.21
  230.1 1.6 collective-permute-done.21
  233.0 6.9 %collective-permute-start.23 = (f32[2,20,2,128]{3,2,1,0:T(2,128)S(1)}, f32[2,20,2,128]{3,2,1,0:T(2,128)S(1)}, u32[]{:S(2)}, u32[]{:S(2)}) collective-permute-start(f32[2,20,2,128]{3,2,1,0:T(2,128)S(1)} %get-tuple-element.37), channel_id=1, source_target_pairs={{0,1},{1,2},{2,3},{3,4},{4,5},{5,6},{6,7},{8,9},{9,10},{10,11},{11... | collective-permute-start | bytes 122888 | tf_op jit(solution)/shard_map/ppermute | solution.py:21
  240.9 16.7 %copy.519 = f32[2,16,32,128]{0,3,2,1:T(8,128)} copy(f32[2,16,32,128]{3,2,1,0:T(8,128)S(1)} %fusion.46) | data formatting | bytes 1048576 | tf_op jit(solution)/shard_map/div | solution.py:86
  257.6 3.0 gather_fusion.5
  260.8 2.0 fusion.34
  264.1 4.9 collective-permute-start.25
  269.3 1.6 collective-permute-done.25
  272.2 6.9 %collective-permute-start.27 = (f32[2,20,2,128]{3,2,1,0:T(2,128)S(1)}, f32[2,20,2,128]{3,2,1,0:T(2,128)S(1)}, u32[]{:S(2)}, u32[]{:S(2)}) collective-permute-start(f32[2,20,2,128]{3,2,1,0:T(2,128)S(1)} %get-tuple-element.33), channel_id=1, source_target_pairs={{0,1},{1,2},{2,3},{3,4},{4,5},{5,6},{6,7},{8,9},{9,10},{10,11},{11... | collective-permute-start | bytes 122888 | tf_op jit(solution)/shard_map/ppermute | solution.py:21
  280.1 16.7 %copy.520 = f32[2,16,32,128]{0,3,2,1:T(8,128)} copy(f32[2,16,32,128]{3,2,1,0:T(8,128)S(1)} %fusion.34) | data formatting | bytes 1048576 | tf_op jit(solution)/shard_map/div | solution.py:86
  296.8 3.0 gather_fusion.6
  299.9 2.0 fusion.22
  303.2 4.9 collective-permute-start.29
  308.4 1.6 collective-permute-done.29
  311.3 7.2 %collective-permute-start.31 = (f32[2,20,2,128]{3,2,1,0:T(2,128)S(1)}, f32[2,20,2,128]{3,2,1,0:T(2,128)S(1)}, u32[]{:S(2)}, u32[]{:S(2)}) collective-permute-start(f32[2,20,2,128]{3,2,1,0:T(2,128)S(1)} %get-tuple-element.29), channel_id=1, source_target_pairs={{0,1},{1,2},{2,3},{3,4},{4,5},{5,6},{6,7},{8,9},{9,10},{10,11},{11... | collective-permute-start | bytes 122888 | tf_op jit(solution)/shard_map/ppermute | solution.py:21
  319.5 16.7 %copy.521 = f32[2,16,32,128]{0,3,2,1:T(8,128)} copy(f32[2,16,32,128]{3,2,1,0:T(8,128)S(1)} %fusion.22) | data formatting | bytes 1048576 | tf_op jit(solution)/shard_map/div | solution.py:86
  336.1 3.0 gather_fusion.7
  339.3 2.0 fusion.10
  341.3 16.8 %copy.522 = f32[2,16,32,128]{0,3,2,1:T(8,128)} copy(f32[2,16,32,128]{3,2,1,0:T(8,128)S(1)} %fusion.10) | data formatting | bytes 1048576 | tf_op jit(solution)/shard_map/div | solution.py:86
  358.1 2.4 gather_fusion.8
  360.5 1.4 bitcast_select_fusion
  362.6 183.4 %psum.7 = f32[1,2,256,8]{2,3,1,0:T(8,128)} all-reduce(f32[1,2,256,8]{2,3,1,0:T(8,128)S(1)} %bitcast.70), channel_id=1, replica_groups=mesh['shot'=4,'gx'=4,'gy'=8] {'gx','gy'}, use_global_device_ids=true, to_apply=%region_1.2 | all-reduce | flops 4096 | bytes 32768 | tf_op jit(solution)/shard_map/psum | solution.py:138
  (124 shorter events, 28.7 us)
Async XLA Ops:
  7.2 97.1 %copy-start.1 = (f32[1,2,16,32,128]{4,3,2,1,0:T(8,128)S(1)}, f32[1,2,16,32,128]{4,3,2,1,0:T(8,128)}, u32[]{:S(2)}) copy-start(f32[1,2,16,32,128]{4,3,2,1,0:T(8,128)} %param.11) | copy-start | bytes 1572868
  7.2 54.9 %all-gather.2.cloned.1.call-start = ((), (), s32[]{:S(2)}) async-start(), calls=%async_computation | async-start | bytes 4456448 | tf_op jit(solution)/shard_map/all_gather | solution.py:113
  8.8 17.0 %collective-permute-start = (f32[2,2,32,128]{3,2,1,0:T(8,128)S(1)}, f32[2,2,32,128]{3,2,1,0:T(8,128)S(1)}, u32[]{:S(2)}, u32[]{:S(2)}) collective-permute-start(f32[2,2,32,128]{3,2,1,0:T(8,128)S(1)} %get-tuple-element.104), channel_id=1, source_target_pairs={{8,0},{16,8},{24,16},{9,1},{17,9},{25,17},{10,2},{18,10},{26,18},{... | collective-permute-start | bytes 196616 | tf_op jit(solution)/shard_map/ppermute | solution.py:23
  10.1 15.8 %collective-permute-start.1 = (f32[2,2,32,128]{3,2,1,0:T(8,128)S(1)}, f32[2,2,32,128]{3,2,1,0:T(8,128)S(1)}, u32[]{:S(2)}, u32[]{:S(2)}) collective-permute-start(f32[2,2,32,128]{3,2,1,0:T(8,128)S(1)} %get-tuple-element.105), channel_id=1, source_target_pairs={{0,8},{8,16},{16,24},{1,9},{9,17},{17,25},{2,10},{10,18},{18,26},{... | collective-permute-start | bytes 196616 | tf_op jit(solution)/shard_map/ppermute | solution.py:21
  25.8 39.0 %copy-start.3 = (f32[2,2,32,128]{3,2,1,0:T(8,128)}, f32[2,2,32,128]{3,2,1,0:T(8,128)S(1)}, u32[]{:S(2)}) copy-start(f32[2,2,32,128]{3,2,1,0:T(8,128)S(1)} %collective-permute-done) | copy-start | bytes 196612
  25.9 39.0 %copy-start.4 = (f32[2,2,32,128]{3,2,1,0:T(8,128)}, f32[2,2,32,128]{3,2,1,0:T(8,128)S(1)}, u32[]{:S(2)}) copy-start(f32[2,2,32,128]{3,2,1,0:T(8,128)S(1)} %collective-permute-done.1) | copy-start | bytes 196612
  26.9 7.7 %collective-permute-start.2 = (f32[2,20,2,128]{3,2,1,0:T(2,128)S(1)}, f32[2,20,2,128]{3,2,1,0:T(2,128)S(1)}, u32[]{:S(2)}, u32[]{:S(2)}) collective-permute-start(f32[2,20,2,128]{3,2,1,0:T(2,128)S(1)} %get-tuple-element.56), channel_id=1, source_target_pairs={{1,0},{2,1},{3,2},{4,3},{5,4},{6,5},{7,6},{9,8},{10,9},{11,10},{12... | collective-permute-start | bytes 122888 | tf_op jit(solution)/shard_map/ppermute | solution.py:23
  28.2 7.9 %collective-permute-start.3 = (f32[2,20,2,128]{3,2,1,0:T(2,128)S(1)}, f32[2,20,2,128]{3,2,1,0:T(2,128)S(1)}, u32[]{:S(2)}, u32[]{:S(2)}) collective-permute-start(f32[2,20,2,128]{3,2,1,0:T(2,128)S(1)} %get-tuple-element.57), channel_id=1, source_target_pairs={{0,1},{1,2},{2,3},{3,4},{4,5},{5,6},{6,7},{8,9},{9,10},{10,11},{11... | collective-permute-start | bytes 122888 | tf_op jit(solution)/shard_map/ppermute | solution.py:21
  68.1 6.8 %collective-permute-start.4 = (f32[2,2,32,128]{3,2,1,0:T(8,128)S(1)}, f32[2,2,32,128]{3,2,1,0:T(8,128)S(1)}, u32[]{:S(2)}, u32[]{:S(2)}) collective-permute-start(f32[2,2,32,128]{3,2,1,0:T(8,128)S(1)} %get-tuple-element.98), channel_id=1, source_target_pairs={{8,0},{16,8},{24,16},{9,1},{17,9},{25,17},{10,2},{18,10},{26,18},{... | collective-permute-start | bytes 196616 | tf_op jit(solution)/shard_map/ppermute | solution.py:23
  69.4 6.7 %collective-permute-start.5 = (f32[2,2,32,128]{3,2,1,0:T(8,128)S(1)}, f32[2,2,32,128]{3,2,1,0:T(8,128)S(1)}, u32[]{:S(2)}, u32[]{:S(2)}) collective-permute-start(f32[2,2,32,128]{3,2,1,0:T(8,128)S(1)} %get-tuple-element.99), channel_id=1, source_target_pairs={{0,8},{8,16},{16,24},{1,9},{9,17},{17,25},{2,10},{10,18},{18,26},{... | collective-permute-start | bytes 196616 | tf_op jit(solution)/shard_map/ppermute | solution.py:21
  76.0 28.2 %copy-start.11 = (f32[2,2,32,128]{3,2,1,0:T(8,128)}, f32[2,2,32,128]{3,2,1,0:T(8,128)S(1)}, u32[]{:S(2)}) copy-start(f32[2,2,32,128]{3,2,1,0:T(8,128)S(1)} %collective-permute-done.5) | copy-start | bytes 196612
  76.1 28.0 %collective-permute-start.6 = (f32[2,20,2,128]{3,2,1,0:T(2,128)S(1)}, f32[2,20,2,128]{3,2,1,0:T(2,128)S(1)}, u32[]{:S(2)}, u32[]{:S(2)}) collective-permute-start(f32[2,20,2,128]{3,2,1,0:T(2,128)S(1)} %get-tuple-element.52), channel_id=1, source_target_pairs={{1,0},{2,1},{3,2},{4,3},{5,4},{6,5},{7,6},{9,8},{10,9},{11,10},{12... | collective-permute-start | bytes 122888 | tf_op jit(solution)/shard_map/ppermute | solution.py:23
  77.4 26.7 %collective-permute-start.7 = (f32[2,20,2,128]{3,2,1,0:T(2,128)S(1)}, f32[2,20,2,128]{3,2,1,0:T(2,128)S(1)}, u32[]{:S(2)}, u32[]{:S(2)}) collective-permute-start(f32[2,20,2,128]{3,2,1,0:T(2,128)S(1)} %get-tuple-element.53), channel_id=1, source_target_pairs={{0,1},{1,2},{2,3},{3,4},{4,5},{5,6},{6,7},{8,9},{9,10},{10,11},{11... | collective-permute-start | bytes 122888 | tf_op jit(solution)/shard_map/ppermute | solution.py:21
  106.2 6.6 %collective-permute-start.8 = (f32[2,2,32,128]{3,2,1,0:T(8,128)S(1)}, f32[2,2,32,128]{3,2,1,0:T(8,128)S(1)}, u32[]{:S(2)}, u32[]{:S(2)}) collective-permute-start(f32[2,2,32,128]{3,2,1,0:T(8,128)S(1)} %get-tuple-element.92), channel_id=1, source_target_pairs={{8,0},{16,8},{24,16},{9,1},{17,9},{25,17},{10,2},{18,10},{26,18},{... | collective-permute-start | bytes 196616 | tf_op jit(solution)/shard_map/ppermute | solution.py:23
  107.5 6.9 %collective-permute-start.9 = (f32[2,2,32,128]{3,2,1,0:T(8,128)S(1)}, f32[2,2,32,128]{3,2,1,0:T(8,128)S(1)}, u32[]{:S(2)}, u32[]{:S(2)}) collective-permute-start(f32[2,2,32,128]{3,2,1,0:T(8,128)S(1)} %get-tuple-element.93), channel_id=1, source_target_pairs={{0,8},{8,16},{16,24},{1,9},{9,17},{17,25},{2,10},{10,18},{18,26},{... | collective-permute-start | bytes 196616 | tf_op jit(solution)/shard_map/ppermute | solution.py:21
  114.4 28.7 %copy-start.6 = (f32[2,2,32,128]{3,2,1,0:T(8,128)}, f32[2,2,32,128]{3,2,1,0:T(8,128)S(1)}, u32[]{:S(2)}) copy-start(f32[2,2,32,128]{3,2,1,0:T(8,128)S(1)} %collective-permute-done.9) | copy-start | bytes 196612
  114.5 28.5 %collective-permute-start.10 = (f32[2,20,2,128]{3,2,1,0:T(2,128)S(1)}, f32[2,20,2,128]{3,2,1,0:T(2,128)S(1)}, u32[]{:S(2)}, u32[]{:S(2)}) collective-permute-start(f32[2,20,2,128]{3,2,1,0:T(2,128)S(1)} %get-tuple-element.48), channel_id=1, source_target_pairs={{1,0},{2,1},{3,2},{4,3},{5,4},{6,5},{7,6},{9,8},{10,9},{11,10},{12... | collective-permute-start | bytes 122888 | tf_op jit(solution)/shard_map/ppermute | solution.py:23
  115.8 27.2 %collective-permute-start.11 = (f32[2,20,2,128]{3,2,1,0:T(2,128)S(1)}, f32[2,20,2,128]{3,2,1,0:T(2,128)S(1)}, u32[]{:S(2)}, u32[]{:S(2)}) collective-permute-start(f32[2,20,2,128]{3,2,1,0:T(2,128)S(1)} %get-tuple-element.49), channel_id=1, source_target_pairs={{0,1},{1,2},{2,3},{3,4},{4,5},{5,6},{6,7},{8,9},{9,10},{10,11},{11... | collective-permute-start | bytes 122888 | tf_op jit(solution)/shard_map/ppermute | solution.py:21
  145.1 6.5 %collective-permute-start.12 = (f32[2,2,32,128]{3,2,1,0:T(8,128)S(1)}, f32[2,2,32,128]{3,2,1,0:T(8,128)S(1)}, u32[]{:S(2)}, u32[]{:S(2)}) collective-permute-start(f32[2,2,32,128]{3,2,1,0:T(8,128)S(1)} %get-tuple-element.86), channel_id=1, source_target_pairs={{8,0},{16,8},{24,16},{9,1},{17,9},{25,17},{10,2},{18,10},{26,18},{... | collective-permute-start | bytes 196616 | tf_op jit(solution)/shard_map/ppermute | solution.py:23
  146.4 6.8 %collective-permute-start.13 = (f32[2,2,32,128]{3,2,1,0:T(8,128)S(1)}, f32[2,2,32,128]{3,2,1,0:T(8,128)S(1)}, u32[]{:S(2)}, u32[]{:S(2)}) collective-permute-start(f32[2,2,32,128]{3,2,1,0:T(8,128)S(1)} %get-tuple-element.87), channel_id=1, source_target_pairs={{0,8},{8,16},{16,24},{1,9},{9,17},{17,25},{2,10},{10,18},{18,26},{... | collective-permute-start | bytes 196616 | tf_op jit(solution)/shard_map/ppermute | solution.py:21
  153.2 29.1 %copy-start.7 = (f32[2,2,32,128]{3,2,1,0:T(8,128)}, f32[2,2,32,128]{3,2,1,0:T(8,128)S(1)}, u32[]{:S(2)}) copy-start(f32[2,2,32,128]{3,2,1,0:T(8,128)S(1)} %collective-permute-done.13) | copy-start | bytes 196612
  153.2 28.9 %collective-permute-start.14 = (f32[2,20,2,128]{3,2,1,0:T(2,128)S(1)}, f32[2,20,2,128]{3,2,1,0:T(2,128)S(1)}, u32[]{:S(2)}, u32[]{:S(2)}) collective-permute-start(f32[2,20,2,128]{3,2,1,0:T(2,128)S(1)} %get-tuple-element.44), channel_id=1, source_target_pairs={{1,0},{2,1},{3,2},{4,3},{5,4},{6,5},{7,6},{9,8},{10,9},{11,10},{12... | collective-permute-start | bytes 122888 | tf_op jit(solution)/shard_map/ppermute | solution.py:23
  154.5 27.6 %collective-permute-start.15 = (f32[2,20,2,128]{3,2,1,0:T(2,128)S(1)}, f32[2,20,2,128]{3,2,1,0:T(2,128)S(1)}, u32[]{:S(2)}, u32[]{:S(2)}) collective-permute-start(f32[2,20,2,128]{3,2,1,0:T(2,128)S(1)} %get-tuple-element.45), channel_id=1, source_target_pairs={{0,1},{1,2},{2,3},{3,4},{4,5},{5,6},{6,7},{8,9},{9,10},{10,11},{11... | collective-permute-start | bytes 122888 | tf_op jit(solution)/shard_map/ppermute | solution.py:21
  184.3 6.5 %collective-permute-start.16 = (f32[2,2,32,128]{3,2,1,0:T(8,128)S(1)}, f32[2,2,32,128]{3,2,1,0:T(8,128)S(1)}, u32[]{:S(2)}, u32[]{:S(2)}) collective-permute-start(f32[2,2,32,128]{3,2,1,0:T(8,128)S(1)} %get-tuple-element.80), channel_id=1, source_target_pairs={{8,0},{16,8},{24,16},{9,1},{17,9},{25,17},{10,2},{18,10},{26,18},{... | collective-permute-start | bytes 196616 | tf_op jit(solution)/shard_map/ppermute | solution.py:23
  185.6 6.8 %collective-permute-start.17 = (f32[2,2,32,128]{3,2,1,0:T(8,128)S(1)}, f32[2,2,32,128]{3,2,1,0:T(8,128)S(1)}, u32[]{:S(2)}, u32[]{:S(2)}) collective-permute-start(f32[2,2,32,128]{3,2,1,0:T(8,128)S(1)} %get-tuple-element.81), channel_id=1, source_target_pairs={{0,8},{8,16},{16,24},{1,9},{9,17},{17,25},{2,10},{10,18},{18,26},{... | collective-permute-start | bytes 196616 | tf_op jit(solution)/shard_map/ppermute | solution.py:21
  192.3 29.3 %copy-start.8 = (f32[2,2,32,128]{3,2,1,0:T(8,128)}, f32[2,2,32,128]{3,2,1,0:T(8,128)S(1)}, u32[]{:S(2)}) copy-start(f32[2,2,32,128]{3,2,1,0:T(8,128)S(1)} %collective-permute-done.17) | copy-start | bytes 196612
  192.4 29.1 %collective-permute-start.18 = (f32[2,20,2,128]{3,2,1,0:T(2,128)S(1)}, f32[2,20,2,128]{3,2,1,0:T(2,128)S(1)}, u32[]{:S(2)}, u32[]{:S(2)}) collective-permute-start(f32[2,20,2,128]{3,2,1,0:T(2,128)S(1)} %get-tuple-element.40), channel_id=1, source_target_pairs={{1,0},{2,1},{3,2},{4,3},{5,4},{6,5},{7,6},{9,8},{10,9},{11,10},{12... | collective-permute-start | bytes 122888 | tf_op jit(solution)/shard_map/ppermute | solution.py:23
  193.7 27.8 %collective-permute-start.19 = (f32[2,20,2,128]{3,2,1,0:T(2,128)S(1)}, f32[2,20,2,128]{3,2,1,0:T(2,128)S(1)}, u32[]{:S(2)}, u32[]{:S(2)}) collective-permute-start(f32[2,20,2,128]{3,2,1,0:T(2,128)S(1)} %get-tuple-element.41), channel_id=1, source_target_pairs={{0,1},{1,2},{2,3},{3,4},{4,5},{5,6},{6,7},{8,9},{9,10},{10,11},{11... | collective-permute-start | bytes 122888 | tf_op jit(solution)/shard_map/ppermute | solution.py:21
  223.6 6.5 %collective-permute-start.20 = (f32[2,2,32,128]{3,2,1,0:T(8,128)S(1)}, f32[2,2,32,128]{3,2,1,0:T(8,128)S(1)}, u32[]{:S(2)}, u32[]{:S(2)}) collective-permute-start(f32[2,2,32,128]{3,2,1,0:T(8,128)S(1)} %get-tuple-element.74), channel_id=1, source_target_pairs={{8,0},{16,8},{24,16},{9,1},{17,9},{25,17},{10,2},{18,10},{26,18},{... | collective-permute-start | bytes 196616 | tf_op jit(solution)/shard_map/ppermute | solution.py:23
  224.9 6.8 %collective-permute-start.21 = (f32[2,2,32,128]{3,2,1,0:T(8,128)S(1)}, f32[2,2,32,128]{3,2,1,0:T(8,128)S(1)}, u32[]{:S(2)}, u32[]{:S(2)}) collective-permute-start(f32[2,2,32,128]{3,2,1,0:T(8,128)S(1)} %get-tuple-element.75), channel_id=1, source_target_pairs={{0,8},{8,16},{16,24},{1,9},{9,17},{17,25},{2,10},{10,18},{18,26},{... | collective-permute-start | bytes 196616 | tf_op jit(solution)/shard_map/ppermute | solution.py:21
  231.7 29.1 %copy-start.9 = (f32[2,2,32,128]{3,2,1,0:T(8,128)}, f32[2,2,32,128]{3,2,1,0:T(8,128)S(1)}, u32[]{:S(2)}) copy-start(f32[2,2,32,128]{3,2,1,0:T(8,128)S(1)} %collective-permute-done.21) | copy-start | bytes 196612
  231.7 28.9 %collective-permute-start.22 = (f32[2,20,2,128]{3,2,1,0:T(2,128)S(1)}, f32[2,20,2,128]{3,2,1,0:T(2,128)S(1)}, u32[]{:S(2)}, u32[]{:S(2)}) collective-permute-start(f32[2,20,2,128]{3,2,1,0:T(2,128)S(1)} %get-tuple-element.36), channel_id=1, source_target_pairs={{1,0},{2,1},{3,2},{4,3},{5,4},{6,5},{7,6},{9,8},{10,9},{11,10},{12... | collective-permute-start | bytes 122888 | tf_op jit(solution)/shard_map/ppermute | solution.py:23
  233.0 27.6 %collective-permute-start.23 = (f32[2,20,2,128]{3,2,1,0:T(2,128)S(1)}, f32[2,20,2,128]{3,2,1,0:T(2,128)S(1)}, u32[]{:S(2)}, u32[]{:S(2)}) collective-permute-start(f32[2,20,2,128]{3,2,1,0:T(2,128)S(1)} %get-tuple-element.37), channel_id=1, source_target_pairs={{0,1},{1,2},{2,3},{3,4},{4,5},{5,6},{6,7},{8,9},{9,10},{10,11},{11... | collective-permute-start | bytes 122888 | tf_op jit(solution)/shard_map/ppermute | solution.py:21
  262.8 6.5 %collective-permute-start.24 = (f32[2,2,32,128]{3,2,1,0:T(8,128)S(1)}, f32[2,2,32,128]{3,2,1,0:T(8,128)S(1)}, u32[]{:S(2)}, u32[]{:S(2)}) collective-permute-start(f32[2,2,32,128]{3,2,1,0:T(8,128)S(1)} %get-tuple-element.68), channel_id=1, source_target_pairs={{8,0},{16,8},{24,16},{9,1},{17,9},{25,17},{10,2},{18,10},{26,18},{... | collective-permute-start | bytes 196616 | tf_op jit(solution)/shard_map/ppermute | solution.py:23
  264.1 6.8 %collective-permute-start.25 = (f32[2,2,32,128]{3,2,1,0:T(8,128)S(1)}, f32[2,2,32,128]{3,2,1,0:T(8,128)S(1)}, u32[]{:S(2)}, u32[]{:S(2)}) collective-permute-start(f32[2,2,32,128]{3,2,1,0:T(8,128)S(1)} %get-tuple-element.69), channel_id=1, source_target_pairs={{0,8},{8,16},{16,24},{1,9},{9,17},{17,25},{2,10},{10,18},{18,26},{... | collective-permute-start | bytes 196616 | tf_op jit(solution)/shard_map/ppermute | solution.py:21
  270.8 29.1 %copy-start.10 = (f32[2,2,32,128]{3,2,1,0:T(8,128)}, f32[2,2,32,128]{3,2,1,0:T(8,128)S(1)}, u32[]{:S(2)}) copy-start(f32[2,2,32,128]{3,2,1,0:T(8,128)S(1)} %collective-permute-done.25) | copy-start | bytes 196612
  270.9 28.9 %collective-permute-start.26 = (f32[2,20,2,128]{3,2,1,0:T(2,128)S(1)}, f32[2,20,2,128]{3,2,1,0:T(2,128)S(1)}, u32[]{:S(2)}, u32[]{:S(2)}) collective-permute-start(f32[2,20,2,128]{3,2,1,0:T(2,128)S(1)} %get-tuple-element.32), channel_id=1, source_target_pairs={{1,0},{2,1},{3,2},{4,3},{5,4},{6,5},{7,6},{9,8},{10,9},{11,10},{12... | collective-permute-start | bytes 122888 | tf_op jit(solution)/shard_map/ppermute | solution.py:23
  272.2 27.6 %collective-permute-start.27 = (f32[2,20,2,128]{3,2,1,0:T(2,128)S(1)}, f32[2,20,2,128]{3,2,1,0:T(2,128)S(1)}, u32[]{:S(2)}, u32[]{:S(2)}) collective-permute-start(f32[2,20,2,128]{3,2,1,0:T(2,128)S(1)} %get-tuple-element.33), channel_id=1, source_target_pairs={{0,1},{1,2},{2,3},{3,4},{4,5},{5,6},{6,7},{8,9},{9,10},{10,11},{11... | collective-permute-start | bytes 122888 | tf_op jit(solution)/shard_map/ppermute | solution.py:21
  301.9 56.2 %copy-start = (f32[2,16,32,128]{3,2,1,0:T(8,128)}, f32[2,16,32,128]{3,2,1,0:T(8,128)S(1)}, u32[]{:S(2)}) copy-start(f32[2,16,32,128]{3,2,1,0:T(8,128)S(1)} %fusion.22) | copy-start | bytes 1572868
  301.9 6.5 %collective-permute-start.28 = (f32[2,2,32,128]{3,2,1,0:T(8,128)S(1)}, f32[2,2,32,128]{3,2,1,0:T(8,128)S(1)}, u32[]{:S(2)}, u32[]{:S(2)}) collective-permute-start(f32[2,2,32,128]{3,2,1,0:T(8,128)S(1)} %get-tuple-element.62), channel_id=1, source_target_pairs={{8,0},{16,8},{24,16},{9,1},{17,9},{25,17},{10,2},{18,10},{26,18},{... | collective-permute-start | bytes 196616 | tf_op jit(solution)/shard_map/ppermute | solution.py:23
  303.2 6.8 %collective-permute-start.29 = (f32[2,2,32,128]{3,2,1,0:T(8,128)S(1)}, f32[2,2,32,128]{3,2,1,0:T(8,128)S(1)}, u32[]{:S(2)}, u32[]{:S(2)}) collective-permute-start(f32[2,2,32,128]{3,2,1,0:T(8,128)S(1)} %get-tuple-element.63), channel_id=1, source_target_pairs={{0,8},{8,16},{16,24},{1,9},{9,17},{17,25},{2,10},{10,18},{18,26},{... | collective-permute-start | bytes 196616 | tf_op jit(solution)/shard_map/ppermute | solution.py:21
  310.0 29.3 %copy-start.5 = (f32[2,2,32,128]{3,2,1,0:T(8,128)}, f32[2,2,32,128]{3,2,1,0:T(8,128)S(1)}, u32[]{:S(2)}) copy-start(f32[2,2,32,128]{3,2,1,0:T(8,128)S(1)} %collective-permute-done.29) | copy-start | bytes 196612
  310.0 29.1 %collective-permute-start.30 = (f32[2,20,2,128]{3,2,1,0:T(2,128)S(1)}, f32[2,20,2,128]{3,2,1,0:T(2,128)S(1)}, u32[]{:S(2)}, u32[]{:S(2)}) collective-permute-start(f32[2,20,2,128]{3,2,1,0:T(2,128)S(1)} %get-tuple-element.28), channel_id=1, source_target_pairs={{1,0},{2,1},{3,2},{4,3},{5,4},{6,5},{7,6},{9,8},{10,9},{11,10},{12... | collective-permute-start | bytes 122888 | tf_op jit(solution)/shard_map/ppermute | solution.py:23
  311.3 27.8 %collective-permute-start.31 = (f32[2,20,2,128]{3,2,1,0:T(2,128)S(1)}, f32[2,20,2,128]{3,2,1,0:T(2,128)S(1)}, u32[]{:S(2)}, u32[]{:S(2)}) collective-permute-start(f32[2,20,2,128]{3,2,1,0:T(2,128)S(1)} %get-tuple-element.29), channel_id=1, source_target_pairs={{0,1},{1,2},{2,3},{3,4},{4,5},{5,6},{6,7},{8,9},{9,10},{10,11},{11... | collective-permute-start | bytes 122888 | tf_op jit(solution)/shard_map/ppermute | solution.py:21
  341.3 204.7 %copy-start.2 = (f32[2,16,32,128]{3,2,1,0:T(8,128)}, f32[2,16,32,128]{3,2,1,0:T(8,128)S(1)}, u32[]{:S(2)}) copy-start(f32[2,16,32,128]{3,2,1,0:T(8,128)S(1)} %fusion.10) | copy-start | bytes 1572868
  341.3 19.2 %copy-start.12 = (f32[256,2]{1,0:T(8,128)S(1)}, f32[256,2]{1,0:T(8,128)}, u32[]{:S(2)}) copy-start(f32[256,2]{1,0:T(8,128)} %gather_fusion.7) | copy-start | bytes 6148
Sparse Core Ops, SparseCore 0:
  9.7 52.3 all-gather.1
where the time goes:
time: 554 us; the launch traced here: 553 us
  blocking collectives  183 us (33%)
  local copies, waits for them, and re-layouts  177 us (32%)
  starting transfers between devices  113 us (20%)
  waiting for transfers between devices  39.1 us (7%)
  other arithmetic  24.3 us (4%)
  between operations  16 us (3%)
    psum x1, blocking collectives, local(): traces = lax.psum(jnp.stack(recorded, axis=-1), ('gx', 'gy'))  183 us
    div x8, local copies, waits for them, and re-layouts, advance(): (2.0 * middle - (1.0 - damp) * previous + coef * laplace(extended) + inje...  134 us
    ppermute x16, starting transfers between devices, extended_2(): lax.ppermute(tail, axis, [(i, (i + 1) % count) for i in range(ends)])  92.2 us
    all_gather x1, waiting for transfers between devices, local(): piece = lax.all_gather(model_tiles, ('shot', 'gx'), axis=0, tiled=True)  24.6 us
    gather x8, local copies, waits for them, and re-layouts, sample(): field[:, jnp.clip(local_x, 0, size_x - 1), jnp.clip(local_y, 0, size_y -...  23.6 us
    ppermute x16, starting transfers between devices, extended_2(): lax.ppermute(head, axis, [((i + 1) % count, i) for i in range(ends)])  20.7 us
    div x8, other arithmetic, advance(): (2.0 * middle - (1.0 - damp) * previous + coef * laplace(extended) + inje...  16.9 us
    slice x16, local copies, waits for them, and re-layouts, depth_ahead(): return jnp.concatenate([field[..., reach:], filler], axis=-1)  12.5 us
  transfers between devices with their start and end apart: 33, of which 17 were waited for; matrix products, arithmetic and copies ran while one was open for 29% of the time, Pallas kernels for 0%

commit v1 on v0

--- a/solution.py
+++ b/solution.py
@@ -135,7 +135,9 @@
         recorded.append(sample(fresh, receiver_cells, x_start, y_start))
         previous = current
         current = fresh
-    traces = lax.psum(jnp.stack(recorded, axis=-1), ("gx", "gy"))
+    traces = jnp.stack(recorded, axis=-1)
+    for mesh_axis in ("gx", "gy"):
+        traces = lax.psum(traces, mesh_axis)
     return (current[None], previous[None], traces[None])
 
 

time: 554 us -> 432 us (0.78)
  blocking collectives: 183 us -> 60.9 us
    psum x1 -> x2, blocking collectives: 183 us -> 60.9 us  [local(): traces = lax.psum(traces, mesh_axis)]
  transfers between devices with their start and end apart: 33 -> 33, of which waited for: 17 -> 17; matrix products, arithmetic and copies ran while one was open for 29% -> 37% of each run, Pallas kernels for 0% -> 0%
where the time goes in v1:
time: 432 us; the launch traced here: 430 us
  local copies, waits for them, and re-layouts  177 us (41%)
  starting transfers between devices  113 us (26%)
  blocking collectives  60.9 us (14%)
  waiting for transfers between devices  39.1 us (9%)
  other arithmetic  24.3 us (6%)
  between operations  16 us (4%)
    div x8, local copies, waits for them, and re-layouts, advance(): (2.0 * middle - (1.0 - damp) * previous + coef * laplace(extended) + inje...  133 us
    ppermute x16, starting transfers between devices, extended_2(): lax.ppermute(tail, axis, [(i, (i + 1) % count) for i in range(ends)])  92.4 us
    psum x2, blocking collectives, local(): traces = lax.psum(traces, mesh_axis)  60.9 us
    all_gather x1, waiting for transfers between devices, local(): piece = lax.all_gather(model_tiles, ('shot', 'gx'), axis=0, tiled=True)  24.6 us
    gather x8, local copies, waits for them, and re-layouts, sample(): field[:, jnp.clip(local_x, 0, size_x - 1), jnp.clip(local_y, 0, size_y -...  23.6 us
    ppermute x16, starting transfers between devices, extended_2(): lax.ppermute(head, axis, [((i + 1) % count, i) for i in range(ends)])  20.7 us
    div x8, other arithmetic, advance(): (2.0 * middle - (1.0 - damp) * previous + coef * laplace(extended) + inje...  16.9 us
    slice x16, local copies, waits for them, and re-layouts, depth_ahead(): return jnp.concatenate([field[..., reach:], filler], axis=-1)  12.5 us
  transfers between devices with their start and end apart: 33, of which 17 were waited for; matrix products, arithmetic and copies ran while one was open for 37% of the time, Pallas kernels for 0%

profile of v1, /device:TPU:0, one launch (start us, length us, event | category | flops | bytes accessed | tf_op | source)
XLA Modules:
  0.0 430.3 jit_solution(9671258919910665084)
XLA Ops:
  8.8 1.3 collective-permute-start
  10.1 4.5 %collective-permute-start.1 = (f32[2,2,32,128]{3,2,1,0:T(8,128)S(1)}, f32[2,2,32,128]{3,2,1,0:T(8,128)S(1)}, u32[]{:S(2)}, u32[]{:S(2)}) collective-permute-start(f32[2,2,32,128]{3,2,1,0:T(8,128)S(1)} %get-tuple-element.105), channel_id=1, source_target_pairs={{0,8},{8,16},{16,24},{1,9},{9,17},{17,25},{2,10},{10,18},{18,26},{... | collective-permute-start | bytes 196616 | tf_op jit(solution)/shard_map/ppermute | solution.py:21
  15.3 1.3 fusion.155
  21.3 2.2 fusion.179
  23.5 2.3 fusion.178
  26.9 1.3 collective-permute-start.2
  28.2 6.1 %collective-permute-start.3 = (f32[2,20,2,128]{3,2,1,0:T(2,128)S(1)}, f32[2,20,2,128]{3,2,1,0:T(2,128)S(1)}, u32[]{:S(2)}, u32[]{:S(2)}) collective-permute-start(f32[2,20,2,128]{3,2,1,0:T(2,128)S(1)} %get-tuple-element.57), channel_id=1, source_target_pairs={{0,1},{1,2},{2,3},{3,4},{4,5},{5,6},{6,7},{8,9},{9,10},{10,11},{11... | collective-permute-start | bytes 122888 | tf_op jit(solution)/shard_map/ppermute | solution.py:21
  34.7 1.5 collective-permute-done.3
  36.1 1.4 pad_maximum_fusion
  37.5 24.6 %all-gather.2.cloned.1.call-done = f32[256,32,128]{2,1,0:T(8,128)} async-done(((f32[16,32,128]{2,1,0:T(8,128)}), f32[256,32,128]{2,1,0:T(8,128)}) %all-gather.2.cloned.1.call-update) | async-done | bytes 4194320 | tf_op jit(solution)/shard_map/all_gather | solution.py:113
  62.1 2.7 gather_fusion
  65.0 3.1 fusion.94
  68.1 1.3 collective-permute-start.4
  69.4 4.5 %collective-permute-start.5 = (f32[2,2,32,128]{3,2,1,0:T(8,128)S(1)}, f32[2,2,32,128]{3,2,1,0:T(8,128)S(1)}, u32[]{:S(2)}, u32[]{:S(2)}) collective-permute-start(f32[2,2,32,128]{3,2,1,0:T(8,128)S(1)} %get-tuple-element.99), channel_id=1, source_target_pairs={{0,8},{8,16},{16,24},{1,9},{9,17},{17,25},{2,10},{10,18},{18,26},{... | collective-permute-start | bytes 196616 | tf_op jit(solution)/shard_map/ppermute | solution.py:21
  76.1 1.3 collective-permute-start.6
  77.4 6.1 %collective-permute-start.7 = (f32[2,20,2,128]{3,2,1,0:T(2,128)S(1)}, f32[2,20,2,128]{3,2,1,0:T(2,128)S(1)}, u32[]{:S(2)}, u32[]{:S(2)}) collective-permute-start(f32[2,20,2,128]{3,2,1,0:T(2,128)S(1)} %get-tuple-element.53), channel_id=1, source_target_pairs={{0,1},{1,2},{2,3},{3,4},{4,5},{5,6},{6,7},{8,9},{9,10},{10,11},{11... | collective-permute-start | bytes 122888 | tf_op jit(solution)/shard_map/ppermute | solution.py:21
  84.4 16.6 %copy.515 = f32[2,16,32,128]{0,3,2,1:T(8,128)} copy(f32[2,16,32,128]{3,2,1,0:T(8,128)S(1)} %fusion.94) | data formatting | bytes 1048576 | tf_op jit(solution)/shard_map/div | solution.py:86
  101.0 3.0 gather_fusion.1
  104.2 2.0 fusion.82
  107.5 5.0 %collective-permute-start.9 = (f32[2,2,32,128]{3,2,1,0:T(8,128)S(1)}, f32[2,2,32,128]{3,2,1,0:T(8,128)S(1)}, u32[]{:S(2)}, u32[]{:S(2)}) collective-permute-start(f32[2,2,32,128]{3,2,1,0:T(8,128)S(1)} %get-tuple-element.93), channel_id=1, source_target_pairs={{0,8},{8,16},{16,24},{1,9},{9,17},{17,25},{2,10},{10,18},{18,26},{... | collective-permute-start | bytes 196616 | tf_op jit(solution)/shard_map/ppermute | solution.py:21
  112.9 1.6 collective-permute-done.9
  115.8 6.5 %collective-permute-start.11 = (f32[2,20,2,128]{3,2,1,0:T(2,128)S(1)}, f32[2,20,2,128]{3,2,1,0:T(2,128)S(1)}, u32[]{:S(2)}, u32[]{:S(2)}) collective-permute-start(f32[2,20,2,128]{3,2,1,0:T(2,128)S(1)} %get-tuple-element.49), channel_id=1, source_target_pairs={{0,1},{1,2},{2,3},{3,4},{4,5},{5,6},{6,7},{8,9},{9,10},{10,11},{11... | collective-permute-start | bytes 122888 | tf_op jit(solution)/shard_map/ppermute | solution.py:21
  123.3 16.6 %copy.516 = f32[2,16,32,128]{0,3,2,1:T(8,128)} copy(f32[2,16,32,128]{3,2,1,0:T(8,128)S(1)} %fusion.82) | data formatting | bytes 1048576 | tf_op jit(solution)/shard_map/div | solution.py:86
  139.9 3.0 gather_fusion.2
  143.1 2.0 fusion.70
  146.4 4.9 %collective-permute-start.13 = (f32[2,2,32,128]{3,2,1,0:T(8,128)S(1)}, f32[2,2,32,128]{3,2,1,0:T(8,128)S(1)}, u32[]{:S(2)}, u32[]{:S(2)}) collective-permute-start(f32[2,2,32,128]{3,2,1,0:T(8,128)S(1)} %get-tuple-element.87), channel_id=1, source_target_pairs={{0,8},{8,16},{16,24},{1,9},{9,17},{17,25},{2,10},{10,18},{18,26},{... | collective-permute-start | bytes 196616 | tf_op jit(solution)/shard_map/ppermute | solution.py:21
  151.6 1.6 collective-permute-done.13
  154.5 7.0 %collective-permute-start.15 = (f32[2,20,2,128]{3,2,1,0:T(2,128)S(1)}, f32[2,20,2,128]{3,2,1,0:T(2,128)S(1)}, u32[]{:S(2)}, u32[]{:S(2)}) collective-permute-start(f32[2,20,2,128]{3,2,1,0:T(2,128)S(1)} %get-tuple-element.45), channel_id=1, source_target_pairs={{0,1},{1,2},{2,3},{3,4},{4,5},{5,6},{6,7},{8,9},{9,10},{10,11},{11... | collective-permute-start | bytes 122888 | tf_op jit(solution)/shard_map/ppermute | solution.py:21
  162.4 16.6 %copy.517 = f32[2,16,32,128]{0,3,2,1:T(8,128)} copy(f32[2,16,32,128]{3,2,1,0:T(8,128)S(1)} %fusion.70) | data formatting | bytes 1048576 | tf_op jit(solution)/shard_map/div | solution.py:86
  179.1 3.0 gather_fusion.3
  182.2 2.0 fusion.58
  184.3 1.3 collective-permute-start.16
  185.6 4.9 %collective-permute-start.17 = (f32[2,2,32,128]{3,2,1,0:T(8,128)S(1)}, f32[2,2,32,128]{3,2,1,0:T(8,128)S(1)}, u32[]{:S(2)}, u32[]{:S(2)}) collective-permute-start(f32[2,2,32,128]{3,2,1,0:T(8,128)S(1)} %get-tuple-element.81), channel_id=1, source_target_pairs={{0,8},{8,16},{16,24},{1,9},{9,17},{17,25},{2,10},{10,18},{18,26},{... | collective-permute-start | bytes 196616 | tf_op jit(solution)/shard_map/ppermute | solution.py:21
  190.8 1.6 collective-permute-done.17
  192.4 1.3 collective-permute-start.18
  193.7 7.1 %collective-permute-start.19 = (f32[2,20,2,128]{3,2,1,0:T(2,128)S(1)}, f32[2,20,2,128]{3,2,1,0:T(2,128)S(1)}, u32[]{:S(2)}, u32[]{:S(2)}) collective-permute-start(f32[2,20,2,128]{3,2,1,0:T(2,128)S(1)} %get-tuple-element.41), channel_id=1, source_target_pairs={{0,1},{1,2},{2,3},{3,4},{4,5},{5,6},{6,7},{8,9},{9,10},{10,11},{11... | collective-permute-start | bytes 122888 | tf_op jit(solution)/shard_map/ppermute | solution.py:21
  201.8 16.6 %copy.518 = f32[2,16,32,128]{0,3,2,1:T(8,128)} copy(f32[2,16,32,128]{3,2,1,0:T(8,128)S(1)} %fusion.58) | data formatting | bytes 1048576 | tf_op jit(solution)/shard_map/div | solution.py:86
  218.4 3.0 gather_fusion.4
  221.6 2.0 fusion.46
  223.6 1.3 collective-permute-start.20
  224.9 4.9 %collective-permute-start.21 = (f32[2,2,32,128]{3,2,1,0:T(8,128)S(1)}, f32[2,2,32,128]{3,2,1,0:T(8,128)S(1)}, u32[]{:S(2)}, u32[]{:S(2)}) collective-permute-start(f32[2,2,32,128]{3,2,1,0:T(8,128)S(1)} %get-tuple-element.75), channel_id=1, source_target_pairs={{0,8},{8,16},{16,24},{1,9},{9,17},{17,25},{2,10},{10,18},{18,26},{... | collective-permute-start | bytes 196616 | tf_op jit(solution)/shard_map/ppermute | solution.py:21
  230.1 1.6 collective-permute-done.21
  233.0 7.0 %collective-permute-start.23 = (f32[2,20,2,128]{3,2,1,0:T(2,128)S(1)}, f32[2,20,2,128]{3,2,1,0:T(2,128)S(1)}, u32[]{:S(2)}, u32[]{:S(2)}) collective-permute-start(f32[2,20,2,128]{3,2,1,0:T(2,128)S(1)} %get-tuple-element.37), channel_id=1, source_target_pairs={{0,1},{1,2},{2,3},{3,4},{4,5},{5,6},{6,7},{8,9},{9,10},{10,11},{11... | collective-permute-start | bytes 122888 | tf_op jit(solution)/shard_map/ppermute | solution.py:21
  240.9 16.6 %copy.519 = f32[2,16,32,128]{0,3,2,1:T(8,128)} copy(f32[2,16,32,128]{3,2,1,0:T(8,128)S(1)} %fusion.46) | data formatting | bytes 1048576 | tf_op jit(solution)/shard_map/div | solution.py:86
  257.6 3.0 gather_fusion.5
  260.8 2.0 fusion.34
  264.1 4.9 %collective-permute-start.25 = (f32[2,2,32,128]{3,2,1,0:T(8,128)S(1)}, f32[2,2,32,128]{3,2,1,0:T(8,128)S(1)}, u32[]{:S(2)}, u32[]{:S(2)}) collective-permute-start(f32[2,2,32,128]{3,2,1,0:T(8,128)S(1)} %get-tuple-element.69), channel_id=1, source_target_pairs={{0,8},{8,16},{16,24},{1,9},{9,17},{17,25},{2,10},{10,18},{18,26},{... | collective-permute-start | bytes 196616 | tf_op jit(solution)/shard_map/ppermute | solution.py:21
  269.3 1.6 collective-permute-done.25
  270.9 1.3 collective-permute-start.26
  272.2 7.0 %collective-permute-start.27 = (f32[2,20,2,128]{3,2,1,0:T(2,128)S(1)}, f32[2,20,2,128]{3,2,1,0:T(2,128)S(1)}, u32[]{:S(2)}, u32[]{:S(2)}) collective-permute-start(f32[2,20,2,128]{3,2,1,0:T(2,128)S(1)} %get-tuple-element.33), channel_id=1, source_target_pairs={{0,1},{1,2},{2,3},{3,4},{4,5},{5,6},{6,7},{8,9},{9,10},{10,11},{11... | collective-permute-start | bytes 122888 | tf_op jit(solution)/shard_map/ppermute | solution.py:21
  280.1 16.6 %copy.520 = f32[2,16,32,128]{0,3,2,1:T(8,128)} copy(f32[2,16,32,128]{3,2,1,0:T(8,128)S(1)} %fusion.34) | data formatting | bytes 1048576 | tf_op jit(solution)/shard_map/div | solution.py:86
  296.8 3.0 gather_fusion.6
  299.9 2.0 fusion.22
  303.3 4.9 %collective-permute-start.29 = (f32[2,2,32,128]{3,2,1,0:T(8,128)S(1)}, f32[2,2,32,128]{3,2,1,0:T(8,128)S(1)}, u32[]{:S(2)}, u32[]{:S(2)}) collective-permute-start(f32[2,2,32,128]{3,2,1,0:T(8,128)S(1)} %get-tuple-element.63), channel_id=1, source_target_pairs={{0,8},{8,16},{16,24},{1,9},{9,17},{17,25},{2,10},{10,18},{18,26},{... | collective-permute-start | bytes 196616 | tf_op jit(solution)/shard_map/ppermute | solution.py:21
  308.5 1.6 collective-permute-done.29
  311.4 7.2 %collective-permute-start.31 = (f32[2,20,2,128]{3,2,1,0:T(2,128)S(1)}, f32[2,20,2,128]{3,2,1,0:T(2,128)S(1)}, u32[]{:S(2)}, u32[]{:S(2)}) collective-permute-start(f32[2,20,2,128]{3,2,1,0:T(2,128)S(1)} %get-tuple-element.29), channel_id=1, source_target_pairs={{0,1},{1,2},{2,3},{3,4},{4,5},{5,6},{6,7},{8,9},{9,10},{10,11},{11... | collective-permute-start | bytes 122888 | tf_op jit(solution)/shard_map/ppermute | solution.py:21
  319.5 16.6 %copy.521 = f32[2,16,32,128]{0,3,2,1:T(8,128)} copy(f32[2,16,32,128]{3,2,1,0:T(8,128)S(1)} %fusion.22) | data formatting | bytes 1048576 | tf_op jit(solution)/shard_map/div | solution.py:86
  336.2 3.0 gather_fusion.7
  339.4 2.0 fusion.10
  341.4 16.7 %copy.522 = f32[2,16,32,128]{0,3,2,1:T(8,128)} copy(f32[2,16,32,128]{3,2,1,0:T(8,128)S(1)} %fusion.10) | data formatting | bytes 1048576 | tf_op jit(solution)/shard_map/div | solution.py:86
  358.1 2.4 gather_fusion.8
  360.5 1.4 bitcast_select_fusion
  362.6 19.1 %psum.14 = f32[2,256,8]{1,2,0:T(8,128)S(1)} all-reduce(f32[2,256,8]{1,2,0:T(8,128)S(1)} %stack.2), channel_id=1, replica_groups=mesh['shot'=4,'gx'=4,'gy'=8] {'gx'}, use_global_device_ids=true, to_apply=%region_1.2 | all-reduce | flops 4096 | bytes 32768 | tf_op jit(solution)/shard_map/psum | solution.py:140
  381.7 41.8 %psum.15 = f32[1,2,256,8]{2,3,1,0:T(8,128)} all-reduce(f32[1,2,256,8]{2,3,1,0:T(8,128)S(1)} %bitcast.70), channel_id=1, replica_groups=mesh['shot'=4,'gx'=4,'gy'=8] {'gy'}, use_global_device_ids=true, to_apply=%region_2.3 | all-reduce | flops 4096 | bytes 32768 | tf_op jit(solution)/shard_map/psum | solution.py:140
  (125 shorter events, 30.0 us)
Async XLA Ops:
  7.2 97.1 %copy-start.1 = (f32[1,2,16,32,128]{4,3,2,1,0:T(8,128)S(1)}, f32[1,2,16,32,128]{4,3,2,1,0:T(8,128)}, u32[]{:S(2)}) copy-start(f32[1,2,16,32,128]{4,3,2,1,0:T(8,128)} %param.11) | copy-start | bytes 1572868
  7.2 54.9 %all-gather.2.cloned.1.call-start = ((), (), s32[]{:S(2)}) async-start(), calls=%async_computation | async-start | bytes 4456448 | tf_op jit(solution)/shard_map/all_gather | solution.py:113
  8.8 17.0 %collective-permute-start = (f32[2,2,32,128]{3,2,1,0:T(8,128)S(1)}, f32[2,2,32,128]{3,2,1,0:T(8,128)S(1)}, u32[]{:S(2)}, u32[]{:S(2)}) collective-permute-start(f32[2,2,32,128]{3,2,1,0:T(8,128)S(1)} %get-tuple-element.104), channel_id=1, source_target_pairs={{8,0},{16,8},{24,16},{9,1},{17,9},{25,17},{10,2},{18,10},{26,18},{... | collective-permute-start | bytes 196616 | tf_op jit(solution)/shard_map/ppermute | solution.py:23
  10.1 15.8 %collective-permute-start.1 = (f32[2,2,32,128]{3,2,1,0:T(8,128)S(1)}, f32[2,2,32,128]{3,2,1,0:T(8,128)S(1)}, u32[]{:S(2)}, u32[]{:S(2)}) collective-permute-start(f32[2,2,32,128]{3,2,1,0:T(8,128)S(1)} %get-tuple-element.105), channel_id=1, source_target_pairs={{0,8},{8,16},{16,24},{1,9},{9,17},{17,25},{2,10},{10,18},{18,26},{... | collective-permute-start | bytes 196616 | tf_op jit(solution)/shard_map/ppermute | solution.py:21
  25.8 39.0 %copy-start.3 = (f32[2,2,32,128]{3,2,1,0:T(8,128)}, f32[2,2,32,128]{3,2,1,0:T(8,128)S(1)}, u32[]{:S(2)}) copy-start(f32[2,2,32,128]{3,2,1,0:T(8,128)S(1)} %collective-permute-done) | copy-start | bytes 196612
  25.9 39.0 %copy-start.4 = (f32[2,2,32,128]{3,2,1,0:T(8,128)}, f32[2,2,32,128]{3,2,1,0:T(8,128)S(1)}, u32[]{:S(2)}) copy-start(f32[2,2,32,128]{3,2,1,0:T(8,128)S(1)} %collective-permute-done.1) | copy-start | bytes 196612
  26.9 7.7 %collective-permute-start.2 = (f32[2,20,2,128]{3,2,1,0:T(2,128)S(1)}, f32[2,20,2,128]{3,2,1,0:T(2,128)S(1)}, u32[]{:S(2)}, u32[]{:S(2)}) collective-permute-start(f32[2,20,2,128]{3,2,1,0:T(2,128)S(1)} %get-tuple-element.56), channel_id=1, source_target_pairs={{1,0},{2,1},{3,2},{4,3},{5,4},{6,5},{7,6},{9,8},{10,9},{11,10},{12... | collective-permute-start | bytes 122888 | tf_op jit(solution)/shard_map/ppermute | solution.py:23
  28.2 7.9 %collective-permute-start.3 = (f32[2,20,2,128]{3,2,1,0:T(2,128)S(1)}, f32[2,20,2,128]{3,2,1,0:T(2,128)S(1)}, u32[]{:S(2)}, u32[]{:S(2)}) collective-permute-start(f32[2,20,2,128]{3,2,1,0:T(2,128)S(1)} %get-tuple-element.57), channel_id=1, source_target_pairs={{0,1},{1,2},{2,3},{3,4},{4,5},{5,6},{6,7},{8,9},{9,10},{10,11},{11... | collective-permute-start | bytes 122888 | tf_op jit(solution)/shard_map/ppermute | solution.py:21
  68.1 6.8 %collective-permute-start.4 = (f32[2,2,32,128]{3,2,1,0:T(8,128)S(1)}, f32[2,2,32,128]{3,2,1,0:T(8,128)S(1)}, u32[]{:S(2)}, u32[]{:S(2)}) collective-permute-start(f32[2,2,32,128]{3,2,1,0:T(8,128)S(1)} %get-tuple-element.98), channel_id=1, source_target_pairs={{8,0},{16,8},{24,16},{9,1},{17,9},{25,17},{10,2},{18,10},{26,18},{... | collective-permute-start | bytes 196616 | tf_op jit(solution)/shard_map/ppermute | solution.py:23
  69.4 6.7 %collective-permute-start.5 = (f32[2,2,32,128]{3,2,1,0:T(8,128)S(1)}, f32[2,2,32,128]{3,2,1,0:T(8,128)S(1)}, u32[]{:S(2)}, u32[]{:S(2)}) collective-permute-start(f32[2,2,32,128]{3,2,1,0:T(8,128)S(1)} %get-tuple-element.99), channel_id=1, source_target_pairs={{0,8},{8,16},{16,24},{1,9},{9,17},{17,25},{2,10},{10,18},{18,26},{... | collective-permute-start | bytes 196616 | tf_op jit(solution)/shard_map/ppermute | solution.py:21
  76.0 28.2 %copy-start.11 = (f32[2,2,32,128]{3,2,1,0:T(8,128)}, f32[2,2,32,128]{3,2,1,0:T(8,128)S(1)}, u32[]{:S(2)}) copy-start(f32[2,2,32,128]{3,2,1,0:T(8,128)S(1)} %collective-permute-done.5) | copy-start | bytes 196612
  76.1 28.0 %collective-permute-start.6 = (f32[2,20,2,128]{3,2,1,0:T(2,128)S(1)}, f32[2,20,2,128]{3,2,1,0:T(2,128)S(1)}, u32[]{:S(2)}, u32[]{:S(2)}) collective-permute-start(f32[2,20,2,128]{3,2,1,0:T(2,128)S(1)} %get-tuple-element.52), channel_id=1, source_target_pairs={{1,0},{2,1},{3,2},{4,3},{5,4},{6,5},{7,6},{9,8},{10,9},{11,10},{12... | collective-permute-start | bytes 122888 | tf_op jit(solution)/shard_map/ppermute | solution.py:23
  77.4 26.7 %collective-permute-start.7 = (f32[2,20,2,128]{3,2,1,0:T(2,128)S(1)}, f32[2,20,2,128]{3,2,1,0:T(2,128)S(1)}, u32[]{:S(2)}, u32[]{:S(2)}) collective-permute-start(f32[2,20,2,128]{3,2,1,0:T(2,128)S(1)} %get-tuple-element.53), channel_id=1, source_target_pairs={{0,1},{1,2},{2,3},{3,4},{4,5},{5,6},{6,7},{8,9},{9,10},{10,11},{11... | collective-permute-start | bytes 122888 | tf_op jit(solution)/shard_map/ppermute | solution.py:21
  106.2 6.6 %collective-permute-start.8 = (f32[2,2,32,128]{3,2,1,0:T(8,128)S(1)}, f32[2,2,32,128]{3,2,1,0:T(8,128)S(1)}, u32[]{:S(2)}, u32[]{:S(2)}) collective-permute-start(f32[2,2,32,128]{3,2,1,0:T(8,128)S(1)} %get-tuple-element.92), channel_id=1, source_target_pairs={{8,0},{16,8},{24,16},{9,1},{17,9},{25,17},{10,2},{18,10},{26,18},{... | collective-permute-start | bytes 196616 | tf_op jit(solution)/shard_map/ppermute | solution.py:23
  107.5 6.9 %collective-permute-start.9 = (f32[2,2,32,128]{3,2,1,0:T(8,128)S(1)}, f32[2,2,32,128]{3,2,1,0:T(8,128)S(1)}, u32[]{:S(2)}, u32[]{:S(2)}) collective-permute-start(f32[2,2,32,128]{3,2,1,0:T(8,128)S(1)} %get-tuple-element.93), channel_id=1, source_target_pairs={{0,8},{8,16},{16,24},{1,9},{9,17},{17,25},{2,10},{10,18},{18,26},{... | collective-permute-start | bytes 196616 | tf_op jit(solution)/shard_map/ppermute | solution.py:21
  114.4 28.6 %copy-start.6 = (f32[2,2,32,128]{3,2,1,0:T(8,128)}, f32[2,2,32,128]{3,2,1,0:T(8,128)S(1)}, u32[]{:S(2)}) copy-start(f32[2,2,32,128]{3,2,1,0:T(8,128)S(1)} %collective-permute-done.9) | copy-start | bytes 196612
  114.5 28.4 %collective-permute-start.10 = (f32[2,20,2,128]{3,2,1,0:T(2,128)S(1)}, f32[2,20,2,128]{3,2,1,0:T(2,128)S(1)}, u32[]{:S(2)}, u32[]{:S(2)}) collective-permute-start(f32[2,20,2,128]{3,2,1,0:T(2,128)S(1)} %get-tuple-element.48), channel_id=1, source_target_pairs={{1,0},{2,1},{3,2},{4,3},{5,4},{6,5},{7,6},{9,8},{10,9},{11,10},{12... | collective-permute-start | bytes 122888 | tf_op jit(solution)/shard_map/ppermute | solution.py:23
  115.8 27.1 %collective-permute-start.11 = (f32[2,20,2,128]{3,2,1,0:T(2,128)S(1)}, f32[2,20,2,128]{3,2,1,0:T(2,128)S(1)}, u32[]{:S(2)}, u32[]{:S(2)}) collective-permute-start(f32[2,20,2,128]{3,2,1,0:T(2,128)S(1)} %get-tuple-element.49), channel_id=1, source_target_pairs={{0,1},{1,2},{2,3},{3,4},{4,5},{5,6},{6,7},{8,9},{9,10},{10,11},{11... | collective-permute-start | bytes 122888 | tf_op jit(solution)/shard_map/ppermute | solution.py:21
  145.1 6.5 %collective-permute-start.12 = (f32[2,2,32,128]{3,2,1,0:T(8,128)S(1)}, f32[2,2,32,128]{3,2,1,0:T(8,128)S(1)}, u32[]{:S(2)}, u32[]{:S(2)}) collective-permute-start(f32[2,2,32,128]{3,2,1,0:T(8,128)S(1)} %get-tuple-element.86), channel_id=1, source_target_pairs={{8,0},{16,8},{24,16},{9,1},{17,9},{25,17},{10,2},{18,10},{26,18},{... | collective-permute-start | bytes 196616 | tf_op jit(solution)/shard_map/ppermute | solution.py:23
  146.4 6.8 %collective-permute-start.13 = (f32[2,2,32,128]{3,2,1,0:T(8,128)S(1)}, f32[2,2,32,128]{3,2,1,0:T(8,128)S(1)}, u32[]{:S(2)}, u32[]{:S(2)}) collective-permute-start(f32[2,2,32,128]{3,2,1,0:T(8,128)S(1)} %get-tuple-element.87), channel_id=1, source_target_pairs={{0,8},{8,16},{16,24},{1,9},{9,17},{17,25},{2,10},{10,18},{18,26},{... | collective-permute-start | bytes 196616 | tf_op jit(solution)/shard_map/ppermute | solution.py:21
  153.2 29.1 %copy-start.7 = (f32[2,2,32,128]{3,2,1,0:T(8,128)}, f32[2,2,32,128]{3,2,1,0:T(8,128)S(1)}, u32[]{:S(2)}) copy-start(f32[2,2,32,128]{3,2,1,0:T(8,128)S(1)} %collective-permute-done.13) | copy-start | bytes 196612
  153.2 28.9 %collective-permute-start.14 = (f32[2,20,2,128]{3,2,1,0:T(2,128)S(1)}, f32[2,20,2,128]{3,2,1,0:T(2,128)S(1)}, u32[]{:S(2)}, u32[]{:S(2)}) collective-permute-start(f32[2,20,2,128]{3,2,1,0:T(2,128)S(1)} %get-tuple-element.44), channel_id=1, source_target_pairs={{1,0},{2,1},{3,2},{4,3},{5,4},{6,5},{7,6},{9,8},{10,9},{11,10},{12... | collective-permute-start | bytes 122888 | tf_op jit(solution)/shard_map/ppermute | solution.py:23
  154.5 27.6 %collective-permute-start.15 = (f32[2,20,2,128]{3,2,1,0:T(2,128)S(1)}, f32[2,20,2,128]{3,2,1,0:T(2,128)S(1)}, u32[]{:S(2)}, u32[]{:S(2)}) collective-permute-start(f32[2,20,2,128]{3,2,1,0:T(2,128)S(1)} %get-tuple-element.45), channel_id=1, source_target_pairs={{0,1},{1,2},{2,3},{3,4},{4,5},{5,6},{6,7},{8,9},{9,10},{10,11},{11... | collective-permute-start | bytes 122888 | tf_op jit(solution)/shard_map/ppermute | solution.py:21
  184.3 6.5 %collective-permute-start.16 = (f32[2,2,32,128]{3,2,1,0:T(8,128)S(1)}, f32[2,2,32,128]{3,2,1,0:T(8,128)S(1)}, u32[]{:S(2)}, u32[]{:S(2)}) collective-permute-start(f32[2,2,32,128]{3,2,1,0:T(8,128)S(1)} %get-tuple-element.80), channel_id=1, source_target_pairs={{8,0},{16,8},{24,16},{9,1},{17,9},{25,17},{10,2},{18,10},{26,18},{... | collective-permute-start | bytes 196616 | tf_op jit(solution)/shard_map/ppermute | solution.py:23
  185.6 6.8 %collective-permute-start.17 = (f32[2,2,32,128]{3,2,1,0:T(8,128)S(1)}, f32[2,2,32,128]{3,2,1,0:T(8,128)S(1)}, u32[]{:S(2)}, u32[]{:S(2)}) collective-permute-start(f32[2,2,32,128]{3,2,1,0:T(8,128)S(1)} %get-tuple-element.81), channel_id=1, source_target_pairs={{0,8},{8,16},{16,24},{1,9},{9,17},{17,25},{2,10},{10,18},{18,26},{... | collective-permute-start | bytes 196616 | tf_op jit(solution)/shard_map/ppermute | solution.py:21
  192.3 29.2 %copy-start.8 = (f32[2,2,32,128]{3,2,1,0:T(8,128)}, f32[2,2,32,128]{3,2,1,0:T(8,128)S(1)}, u32[]{:S(2)}) copy-start(f32[2,2,32,128]{3,2,1,0:T(8,128)S(1)} %collective-permute-done.17) | copy-start | bytes 196612
  192.4 29.1 %collective-permute-start.18 = (f32[2,20,2,128]{3,2,1,0:T(2,128)S(1)}, f32[2,20,2,128]{3,2,1,0:T(2,128)S(1)}, u32[]{:S(2)}, u32[]{:S(2)}) collective-permute-start(f32[2,20,2,128]{3,2,1,0:T(2,128)S(1)} %get-tuple-element.40), channel_id=1, source_target_pairs={{1,0},{2,1},{3,2},{4,3},{5,4},{6,5},{7,6},{9,8},{10,9},{11,10},{12... | collective-permute-start | bytes 122888 | tf_op jit(solution)/shard_map/ppermute | solution.py:23
  193.7 27.8 %collective-permute-start.19 = (f32[2,20,2,128]{3,2,1,0:T(2,128)S(1)}, f32[2,20,2,128]{3,2,1,0:T(2,128)S(1)}, u32[]{:S(2)}, u32[]{:S(2)}) collective-permute-start(f32[2,20,2,128]{3,2,1,0:T(2,128)S(1)} %get-tuple-element.41), channel_id=1, source_target_pairs={{0,1},{1,2},{2,3},{3,4},{4,5},{5,6},{6,7},{8,9},{9,10},{10,11},{11... | collective-permute-start | bytes 122888 | tf_op jit(solution)/shard_map/ppermute | solution.py:21
  223.6 6.5 %collective-permute-start.20 = (f32[2,2,32,128]{3,2,1,0:T(8,128)S(1)}, f32[2,2,32,128]{3,2,1,0:T(8,128)S(1)}, u32[]{:S(2)}, u32[]{:S(2)}) collective-permute-start(f32[2,2,32,128]{3,2,1,0:T(8,128)S(1)} %get-tuple-element.74), channel_id=1, source_target_pairs={{8,0},{16,8},{24,16},{9,1},{17,9},{25,17},{10,2},{18,10},{26,18},{... | collective-permute-start | bytes 196616 | tf_op jit(solution)/shard_map/ppermute | solution.py:23
  224.9 6.8 %collective-permute-start.21 = (f32[2,2,32,128]{3,2,1,0:T(8,128)S(1)}, f32[2,2,32,128]{3,2,1,0:T(8,128)S(1)}, u32[]{:S(2)}, u32[]{:S(2)}) collective-permute-start(f32[2,2,32,128]{3,2,1,0:T(8,128)S(1)} %get-tuple-element.75), channel_id=1, source_target_pairs={{0,8},{8,16},{16,24},{1,9},{9,17},{17,25},{2,10},{10,18},{18,26},{... | collective-permute-start | bytes 196616 | tf_op jit(solution)/shard_map/ppermute | solution.py:21
  231.7 29.1 %copy-start.9 = (f32[2,2,32,128]{3,2,1,0:T(8,128)}, f32[2,2,32,128]{3,2,1,0:T(8,128)S(1)}, u32[]{:S(2)}) copy-start(f32[2,2,32,128]{3,2,1,0:T(8,128)S(1)} %collective-permute-done.21) | copy-start | bytes 196612
  231.7 28.9 %collective-permute-start.22 = (f32[2,20,2,128]{3,2,1,0:T(2,128)S(1)}, f32[2,20,2,128]{3,2,1,0:T(2,128)S(1)}, u32[]{:S(2)}, u32[]{:S(2)}) collective-permute-start(f32[2,20,2,128]{3,2,1,0:T(2,128)S(1)} %get-tuple-element.36), channel_id=1, source_target_pairs={{1,0},{2,1},{3,2},{4,3},{5,4},{6,5},{7,6},{9,8},{10,9},{11,10},{12... | collective-permute-start | bytes 122888 | tf_op jit(solution)/shard_map/ppermute | solution.py:23
  233.0 27.6 %collective-permute-start.23 = (f32[2,20,2,128]{3,2,1,0:T(2,128)S(1)}, f32[2,20,2,128]{3,2,1,0:T(2,128)S(1)}, u32[]{:S(2)}, u32[]{:S(2)}) collective-permute-start(f32[2,20,2,128]{3,2,1,0:T(2,128)S(1)} %get-tuple-element.37), channel_id=1, source_target_pairs={{0,1},{1,2},{2,3},{3,4},{4,5},{5,6},{6,7},{8,9},{9,10},{10,11},{11... | collective-permute-start | bytes 122888 | tf_op jit(solution)/shard_map/ppermute | solution.py:21
  262.8 6.5 %collective-permute-start.24 = (f32[2,2,32,128]{3,2,1,0:T(8,128)S(1)}, f32[2,2,32,128]{3,2,1,0:T(8,128)S(1)}, u32[]{:S(2)}, u32[]{:S(2)}) collective-permute-start(f32[2,2,32,128]{3,2,1,0:T(8,128)S(1)} %get-tuple-element.68), channel_id=1, source_target_pairs={{8,0},{16,8},{24,16},{9,1},{17,9},{25,17},{10,2},{18,10},{26,18},{... | collective-permute-start | bytes 196616 | tf_op jit(solution)/shard_map/ppermute | solution.py:23
  264.1 6.8 %collective-permute-start.25 = (f32[2,2,32,128]{3,2,1,0:T(8,128)S(1)}, f32[2,2,32,128]{3,2,1,0:T(8,128)S(1)}, u32[]{:S(2)}, u32[]{:S(2)}) collective-permute-start(f32[2,2,32,128]{3,2,1,0:T(8,128)S(1)} %get-tuple-element.69), channel_id=1, source_target_pairs={{0,8},{8,16},{16,24},{1,9},{9,17},{17,25},{2,10},{10,18},{18,26},{... | collective-permute-start | bytes 196616 | tf_op jit(solution)/shard_map/ppermute | solution.py:21
  270.9 29.1 %copy-start.10 = (f32[2,2,32,128]{3,2,1,0:T(8,128)}, f32[2,2,32,128]{3,2,1,0:T(8,128)S(1)}, u32[]{:S(2)}) copy-start(f32[2,2,32,128]{3,2,1,0:T(8,128)S(1)} %collective-permute-done.25) | copy-start | bytes 196612
  270.9 28.9 %collective-permute-start.26 = (f32[2,20,2,128]{3,2,1,0:T(2,128)S(1)}, f32[2,20,2,128]{3,2,1,0:T(2,128)S(1)}, u32[]{:S(2)}, u32[]{:S(2)}) collective-permute-start(f32[2,20,2,128]{3,2,1,0:T(2,128)S(1)} %get-tuple-element.32), channel_id=1, source_target_pairs={{1,0},{2,1},{3,2},{4,3},{5,4},{6,5},{7,6},{9,8},{10,9},{11,10},{12... | collective-permute-start | bytes 122888 | tf_op jit(solution)/shard_map/ppermute | solution.py:23
  272.2 27.6 %collective-permute-start.27 = (f32[2,20,2,128]{3,2,1,0:T(2,128)S(1)}, f32[2,20,2,128]{3,2,1,0:T(2,128)S(1)}, u32[]{:S(2)}, u32[]{:S(2)}) collective-permute-start(f32[2,20,2,128]{3,2,1,0:T(2,128)S(1)} %get-tuple-element.33), channel_id=1, source_target_pairs={{0,1},{1,2},{2,3},{3,4},{4,5},{5,6},{6,7},{8,9},{9,10},{10,11},{11... | collective-permute-start | bytes 122888 | tf_op jit(solution)/shard_map/ppermute | solution.py:21
  301.9 56.1 %copy-start = (f32[2,16,32,128]{3,2,1,0:T(8,128)}, f32[2,16,32,128]{3,2,1,0:T(8,128)S(1)}, u32[]{:S(2)}) copy-start(f32[2,16,32,128]{3,2,1,0:T(8,128)S(1)} %fusion.22) | copy-start | bytes 1572868
  302.0 6.5 %collective-permute-start.28 = (f32[2,2,32,128]{3,2,1,0:T(8,128)S(1)}, f32[2,2,32,128]{3,2,1,0:T(8,128)S(1)}, u32[]{:S(2)}, u32[]{:S(2)}) collective-permute-start(f32[2,2,32,128]{3,2,1,0:T(8,128)S(1)} %get-tuple-element.62), channel_id=1, source_target_pairs={{8,0},{16,8},{24,16},{9,1},{17,9},{25,17},{10,2},{18,10},{26,18},{... | collective-permute-start | bytes 196616 | tf_op jit(solution)/shard_map/ppermute | solution.py:23
  303.3 6.8 %collective-permute-start.29 = (f32[2,2,32,128]{3,2,1,0:T(8,128)S(1)}, f32[2,2,32,128]{3,2,1,0:T(8,128)S(1)}, u32[]{:S(2)}, u32[]{:S(2)}) collective-permute-start(f32[2,2,32,128]{3,2,1,0:T(8,128)S(1)} %get-tuple-element.63), channel_id=1, source_target_pairs={{0,8},{8,16},{16,24},{1,9},{9,17},{17,25},{2,10},{10,18},{18,26},{... | collective-permute-start | bytes 196616 | tf_op jit(solution)/shard_map/ppermute | solution.py:21
  310.1 29.3 %copy-start.5 = (f32[2,2,32,128]{3,2,1,0:T(8,128)}, f32[2,2,32,128]{3,2,1,0:T(8,128)S(1)}, u32[]{:S(2)}) copy-start(f32[2,2,32,128]{3,2,1,0:T(8,128)S(1)} %collective-permute-done.29) | copy-start | bytes 196612
  310.1 29.1 %collective-permute-start.30 = (f32[2,20,2,128]{3,2,1,0:T(2,128)S(1)}, f32[2,20,2,128]{3,2,1,0:T(2,128)S(1)}, u32[]{:S(2)}, u32[]{:S(2)}) collective-permute-start(f32[2,20,2,128]{3,2,1,0:T(2,128)S(1)} %get-tuple-element.28), channel_id=1, source_target_pairs={{1,0},{2,1},{3,2},{4,3},{5,4},{6,5},{7,6},{9,8},{10,9},{11,10},{12... | collective-permute-start | bytes 122888 | tf_op jit(solution)/shard_map/ppermute | solution.py:23
  311.4 27.8 %collective-permute-start.31 = (f32[2,20,2,128]{3,2,1,0:T(2,128)S(1)}, f32[2,20,2,128]{3,2,1,0:T(2,128)S(1)}, u32[]{:S(2)}, u32[]{:S(2)}) collective-permute-start(f32[2,20,2,128]{3,2,1,0:T(2,128)S(1)} %get-tuple-element.29), channel_id=1, source_target_pairs={{0,1},{1,2},{2,3},{3,4},{4,5},{5,6},{6,7},{8,9},{9,10},{10,11},{11... | collective-permute-start | bytes 122888 | tf_op jit(solution)/shard_map/ppermute | solution.py:21
  341.3 82.1 %copy-start.2 = (f32[2,16,32,128]{3,2,1,0:T(8,128)}, f32[2,16,32,128]{3,2,1,0:T(8,128)S(1)}, u32[]{:S(2)}) copy-start(f32[2,16,32,128]{3,2,1,0:T(8,128)S(1)} %fusion.10) | copy-start | bytes 1572868
  341.4 19.1 %copy-start.12 = (f32[256,2]{1,0:T(8,128)S(1)}, f32[256,2]{1,0:T(8,128)}, u32[]{:S(2)}) copy-start(f32[256,2]{1,0:T(8,128)} %gather_fusion.7) | copy-start | bytes 6148
Sparse Core Ops, SparseCore 0:
  9.7 52.3 all-gather.1
